TPU v7x, 512 devices: a whole 4x8x8 slice. The times are simulated.
512 devices in a mesh: view: 32 (over x, z), slab: 16 (over y, core).
Axes of the slice: x: 4, y: 8, z: 8, core: 2. Of those that a mesh axis runs over, the one named last changes fastest.
Arguments:
- leaf_coeffs: float32 [64, 256, 768], P('view', 'slab'), may hold values from -6 to 6
- measured: float32 [64, 256, 768], P('view', 'slab'), may hold values from -6 to 6
- ray_weight: float32 [64, 256, 768], P('view', 'slab'), may hold values from 0.25 to 1
- cone_weight: float32 [64, 9], P('view'), may hold values from 0.1 to 0.5
- interp_weight: float32 [5, 2, 64, 4], replicated, may hold values from -2 to 2
- shift_offset: int32 [5, 2, 64], replicated, may hold values from -24 to 24
- source_view: int32 [5, 2, 64], replicated, may hold values from 0 to 1
Outputs:
- residual: float32 [64, 256, 768], P('view', 'slab')
- updated: float32 [64, 256, 768], P('view', 'slab')
Inputs may be any that keep to these rules, and one draw needn't show every extreme that they name: source_view[l, c, v] is a view row within the supplying block.
All inputs are finite; a program needn't handle non-finite values.
Results may differ from a plain program's by a relative error of at most 0.00012.
Values sent between devices are 32-bit elements; how exact they have to be, the bound alone decides.
A program may use at most 64 MiB of HBM per device.

v0:
```python
import jax
import jax.numpy as jnp
from jax import lax
from jax.sharding import PartitionSpec as P

TAPS = 4
SHIFT = 24


def from_partner(x, axis, apart):
    return lax.ppermute(x, axis, [(i, i ^ 1 << apart) for i in range(lax.axis_size(axis))])


def extended(block, sides, width):
    for axis, dim in sides:
        count = lax.axis_size(axis)
        forward = [(i, i + 1) for i in range(count - 1)]
        backward = [(target, source) for source, target in forward]
        low = lax.ppermute(
            lax.slice_in_dim(block, block.shape[dim] - width, None, axis=dim), axis, forward
        )
        high = lax.ppermute(lax.slice_in_dim(block, 0, width, axis=dim), axis, backward)
        block = jnp.concatenate([low, block, high], axis=dim)
    return block


def level_params(
    interp_weight, shift_offset, source_view, level_index, channel, device, view_count
):
    first_row = device * view_count
    tap_weights = lax.dynamic_slice_in_dim(
        interp_weight[level_index, channel], first_row, view_count, 0
    )
    tap_offsets = lax.dynamic_slice_in_dim(
        shift_offset[level_index, channel], first_row, view_count, 0
    )
    chosen_rows = lax.dynamic_slice_in_dim(
        source_view[level_index, channel], first_row, view_count, 0
    )
    return (tap_weights, tap_offsets, chosen_rows)


def row_selector(chosen_rows, view_count):
    return (chosen_rows[:, None] == lax.iota(jnp.int32, view_count)[None, :]).astype(jnp.float32)


def shift_taps(padded, tap_weights, begins, columns, forward):
    tap_count = tap_weights.shape[1]
    outputs = []
    for row_index in range(padded.shape[0]):
        window = lax.dynamic_slice_in_dim(
            padded[row_index], begins[row_index], columns + tap_count - 1, 1
        )
        summed = jnp.zeros((padded.shape[1], columns), jnp.float32)
        for tap_index in range(tap_count):
            offset_in = tap_index if forward else tap_count - 1 - tap_index
            summed = (
                summed
                + tap_weights[row_index, tap_index] * window[:, offset_in : offset_in + columns]
            )
        outputs.append(summed)
    return jnp.stack(outputs)


def resample(source_block, level_terms):
    tap_weights, tap_offsets, chosen_rows = level_terms
    view_count = source_block.shape[0]
    columns = source_block.shape[2]
    margin = SHIFT + TAPS
    selector = row_selector(chosen_rows, view_count)
    picked = jnp.einsum("vm,mzw->vzw", selector, source_block, precision=lax.Precision.HIGHEST)
    padded = jnp.pad(picked, ((0, 0), (0, 0), (margin, margin)))
    begins = tap_offsets + margin
    return shift_taps(padded, tap_weights, begins, columns, True)


def spread_back(cotangent, level_terms):
    tap_weights, tap_offsets, chosen_rows = level_terms
    view_count = cotangent.shape[0]
    columns = cotangent.shape[2]
    margin = SHIFT + TAPS
    padded = jnp.pad(cotangent, ((0, 0), (0, 0), (margin, margin)))
    begins = margin - tap_offsets - (tap_weights.shape[1] - 1)
    accumulated = shift_taps(padded, tap_weights, begins, columns, False)
    selector = row_selector(chosen_rows, view_count)
    return jnp.einsum("vm,vzw->mzw", selector, accumulated, precision=lax.Precision.HIGHEST)


def tilt_forward(padded, cone_weight, output_planes):
    accumulated = jnp.zeros((padded.shape[0], output_planes, padded.shape[2]), jnp.float32)
    for cone_index in range(cone_weight.shape[1]):
        accumulated = (
            accumulated
            + cone_weight[:, cone_index][:, None, None]
            * padded[:, cone_index : cone_index + output_planes]
        )
    return accumulated


def tilt_adjoint(padded, cone_weight, output_planes):
    widest = cone_weight.shape[1] - 1
    accumulated = jnp.zeros((padded.shape[0], output_planes, padded.shape[2]), jnp.float32)
    for cone_index in range(cone_weight.shape[1]):
        begin_at = widest - cone_index
        accumulated = (
            accumulated
            + cone_weight[:, cone_index][:, None, None]
            * padded[:, begin_at : begin_at + output_planes]
        )
    return accumulated


def body(leaf_coeffs, measured, ray_weight, cone_weight, interp_weight, shift_offset, source_view):
    view_count = leaf_coeffs.shape[0]
    planes = leaf_coeffs.shape[1]
    reach_planes = (cone_weight.shape[1] - 1) // 2
    level_count = lax.axis_size("view").bit_length() - 1
    device = lax.axis_index("view")
    current = leaf_coeffs
    for level_index in range(level_count):
        stride = 2**level_index
        partner = device + stride - 2 * stride * (device // stride % 2)
        own_terms = level_params(
            interp_weight, shift_offset, source_view, level_index, 0, device, view_count
        )
        received = from_partner(current, "view", level_index)
        far_terms = level_params(
            interp_weight, shift_offset, source_view, level_index, 1, device, view_count
        )
        current = resample(current, own_terms) + resample(received, far_terms)
    padded = extended(current, (("slab", 1),), reach_planes)
    projection = tilt_forward(padded, cone_weight, planes)
    residual = measured - projection
    weighted = ray_weight * residual
    padded_back = extended(weighted, (("slab", 1),), reach_planes)
    cotangent = tilt_adjoint(padded_back, cone_weight, planes)
    for level_index in reversed(range(level_count)):
        stride = 2**level_index
        partner = device + stride - 2 * stride * (device // stride % 2)
        own_terms = level_params(
            interp_weight, shift_offset, source_view, level_index, 0, device, view_count
        )
        received = from_partner(cotangent, "view", level_index)
        far_terms = level_params(
            interp_weight, shift_offset, source_view, level_index, 1, partner, view_count
        )
        cotangent = spread_back(cotangent, own_terms) + spread_back(received, far_terms)
    updated = leaf_coeffs + cotangent
    return (residual, updated)


def solution(mesh):
    in_specs = (
        P("view", "slab", None),
        P("view", "slab", None),
        P("view", "slab", None),
        P("view", None),
        P(),
        P(),
        P(),
    )
    out_specs = (P("view", "slab", None), P("view", "slab", None))
    return jax.shard_map(body, mesh=mesh, in_specs=in_specs, out_specs=out_specs, check_vma=False)
```

profile of v0, /device:TPU:34, one launch (start us, length us, event | category | flops | bytes accessed | tf_op | source)
XLA Modules:
  0.0 289.3 jit_solution(79074491317421151)
XLA Ops:
  1.6 4.3 %collective-permute-start = (f32[2,16,768]{2,0,1:T(2,128)S(1)}, f32[2,16,768]{2,0,1:T(2,128)S(1)}, u32[]{:S(2)}, u32[]{:S(2)}) collective-permute-start(f32[2,16,768]{2,0,1:T(2,128)S(1)} %copy.15), channel_id=1, source_target_pairs={{0,16},{16,0},{32,48},{48,32},{64,80},{80,64},{96,112},{112,96},{1... | collective-permute-start | bytes 294920 | tf_op jit(solution)/shard_map/ppermute | solution.py:11
  76.9 2.6 fusion.184
  79.8 2.6 fusion.187
  82.6 6.1 %collective-permute-start.1 = (f32[2,16,768]{2,0,1:T(2,128)S(1)}, f32[2,16,768]{2,0,1:T(2,128)S(1)}, u32[]{:S(2)}, u32[]{:S(2)}) collective-permute-start(f32[2,16,768]{2,0,1:T(2,128)S(1)} %maximum_add_fusion), channel_id=1, source_target_pairs={{0,32},{16,48},{32,0},{48,16},{64,96},{80,112},{96,64},{112,80},{1... | collective-permute-start | bytes 294920 | tf_op jit(solution)/shard_map/ppermute | solution.py:11
  89.8 2.6 fusion.177
  101.5 8.2 %collective-permute-start.2 = (f32[2,16,768]{2,0,1:T(2,128)S(1)}, f32[2,16,768]{2,0,1:T(2,128)S(1)}, u32[]{:S(2)}, u32[]{:S(2)}) collective-permute-start(f32[2,16,768]{2,0,1:T(2,128)S(1)} %maximum_add_fusion.1), channel_id=1, source_target_pairs={{0,64},{16,80},{32,96},{48,112},{64,0},{80,16},{96,32},{112,48},{1... | collective-permute-start | bytes 294920 | tf_op jit(solution)/shard_map/ppermute | solution.py:11
  119.7 2.6 fusion.161
  128.8 2.6 fusion.155
  138.0 4.5 %collective-permute-start.4 = (f32[2,16,768]{2,0,1:T(2,128)S(1)}, f32[2,16,768]{2,0,1:T(2,128)S(1)}, u32[]{:S(2)}, u32[]{:S(2)}) collective-permute-start(f32[2,16,768]{2,0,1:T(2,128)S(1)} %maximum_add_fusion.3), channel_id=1, source_target_pairs={{0,256},{16,272},{32,288},{48,304},{64,320},{80,336},{96,352},{112... | collective-permute-start | bytes 294920 | tf_op jit(solution)/shard_map/ppermute | solution.py:11
  152.4 2.6 fusion.134
  160.2 3.3 %collective-permute-done.5 = f32[2,4,768]{2,1,0:T(4,128)S(1)} collective-permute-done((f32[2,4,768]{2,1,0:T(4,128)S(1)}, f32[2,4,768]{2,1,0:T(4,128)S(1)}, u32[]{:S(2)}, u32[]{:S(2)}) %collective-permute-start.5) | collective-permute-done | bytes 24608 | tf_op jit(solution)/shard_map/ppermute | solution.py:19
  166.3 4.9 %collective-permute-start.7 = (f32[2,4,768]{2,1,0:T(4,128)S(1)}, f32[2,4,768]{2,1,0:T(4,128)S(1)}, u32[]{:S(2)}, u32[]{:S(2)}) collective-permute-start(f32[2,4,768]{2,1,0:T(4,128)S(1)} %get-tuple-element.35), channel_id=1, source_target_pairs={{1,0},{2,1},{3,2},{4,3},{5,4},{6,5},{7,6},{8,7},{9,8},{10,9},{11,1... | collective-permute-start | bytes 73736 | tf_op jit(solution)/shard_map/ppermute | solution.py:22
  208.9 3.0 %collective-permute-start.9 = (f32[2,16,768]{2,1,0:T(8,128)S(1)}, f32[2,16,768]{2,1,0:T(8,128)S(1)}, u32[]{:S(2)}, u32[]{:S(2)}) collective-permute-start(f32[2,16,768]{2,1,0:T(8,128)S(1)} %fusion.4), channel_id=1, source_target_pairs={{0,256},{16,272},{32,288},{48,304},{64,320},{80,336},{96,352},{112... | collective-permute-start | bytes 294920 | tf_op jit(solution)/shard_map/ppermute | solution.py:11
  223.9 3.4 %collective-permute-start.10 = (f32[2,16,768]{2,0,1:T(2,128)S(1)}, f32[2,16,768]{2,0,1:T(2,128)S(1)}, u32[]{:S(2)}, u32[]{:S(2)}) collective-permute-start(f32[2,16,768]{2,0,1:T(2,128)S(1)} %convolution_add_fusion.4), channel_id=1, source_target_pairs={{0,128},{16,144},{32,160},{48,176},{64,192},{80,208},{96,224},{112... | collective-permute-start | bytes 294920 | tf_op jit(solution)/shard_map/ppermute | solution.py:11
  230.3 2.6 fusion.113
  233.8 2.7 fusion.102
  236.8 2.7 fusion.105
  240.2 4.4 %collective-permute-start.11 = (f32[2,16,768]{2,0,1:T(2,128)S(1)}, f32[2,16,768]{2,0,1:T(2,128)S(1)}, u32[]{:S(2)}, u32[]{:S(2)}) collective-permute-start(f32[2,16,768]{2,0,1:T(2,128)S(1)} %convolution_add_fusion.3), channel_id=1, source_target_pairs={{0,64},{16,80},{32,96},{48,112},{64,0},{80,16},{96,32},{112,48},{1... | collective-permute-start | bytes 294920 | tf_op jit(solution)/shard_map/ppermute | solution.py:11
  254.0 2.6 fusion.91
  257.4 3.7 %collective-permute-start.12 = (f32[2,16,768]{2,0,1:T(2,128)S(1)}, f32[2,16,768]{2,0,1:T(2,128)S(1)}, u32[]{:S(2)}, u32[]{:S(2)}) collective-permute-start(f32[2,16,768]{2,0,1:T(2,128)S(1)} %convolution_add_fusion.2), channel_id=1, source_target_pairs={{0,32},{16,48},{32,0},{48,16},{64,96},{80,112},{96,64},{112,80},{1... | collective-permute-start | bytes 294920 | tf_op jit(solution)/shard_map/ppermute | solution.py:11
  261.3 2.6 fusion.81
  270.4 2.6 fusion.77
  279.2 2.6 fusion.71
  285.5 2.6 fusion.63
  (287 shorter events, 129.6 us)
Async XLA Ops:
  1.6 74.4 %collective-permute-start = (f32[2,16,768]{2,0,1:T(2,128)S(1)}, f32[2,16,768]{2,0,1:T(2,128)S(1)}, u32[]{:S(2)}, u32[]{:S(2)}) collective-permute-start(f32[2,16,768]{2,0,1:T(2,128)S(1)} %copy.15), channel_id=1, source_target_pairs={{0,16},{16,0},{32,48},{48,32},{64,80},{80,64},{96,112},{112,96},{1... | collective-permute-start | bytes 294920 | tf_op jit(solution)/shard_map/ppermute | solution.py:11
  5.9 0.7 copy-start.4
  36.7 1.9 copy-start.5
  40.2 0.7 copy-start.3
  54.1 1.5 copy-start.2
  82.6 12.5 %collective-permute-start.1 = (f32[2,16,768]{2,0,1:T(2,128)S(1)}, f32[2,16,768]{2,0,1:T(2,128)S(1)}, u32[]{:S(2)}, u32[]{:S(2)}) collective-permute-start(f32[2,16,768]{2,0,1:T(2,128)S(1)} %maximum_add_fusion), channel_id=1, source_target_pairs={{0,32},{16,48},{32,0},{48,16},{64,96},{80,112},{96,64},{112,80},{1... | collective-permute-start | bytes 294920 | tf_op jit(solution)/shard_map/ppermute | solution.py:11
  101.5 14.5 %collective-permute-start.2 = (f32[2,16,768]{2,0,1:T(2,128)S(1)}, f32[2,16,768]{2,0,1:T(2,128)S(1)}, u32[]{:S(2)}, u32[]{:S(2)}) collective-permute-start(f32[2,16,768]{2,0,1:T(2,128)S(1)} %maximum_add_fusion.1), channel_id=1, source_target_pairs={{0,64},{16,80},{32,96},{48,112},{64,0},{80,16},{96,32},{112,48},{1... | collective-permute-start | bytes 294920 | tf_op jit(solution)/shard_map/ppermute | solution.py:11
  122.6 8.9 %collective-permute-start.3 = (f32[2,16,768]{2,0,1:T(2,128)S(1)}, f32[2,16,768]{2,0,1:T(2,128)S(1)}, u32[]{:S(2)}, u32[]{:S(2)}) collective-permute-start(f32[2,16,768]{2,0,1:T(2,128)S(1)} %maximum_add_fusion.2), channel_id=1, source_target_pairs={{0,128},{16,144},{32,160},{48,176},{64,192},{80,208},{96,224},{112... | collective-permute-start | bytes 294920 | tf_op jit(solution)/shard_map/ppermute | solution.py:11
  138.0 10.8 %collective-permute-start.4 = (f32[2,16,768]{2,0,1:T(2,128)S(1)}, f32[2,16,768]{2,0,1:T(2,128)S(1)}, u32[]{:S(2)}, u32[]{:S(2)}) collective-permute-start(f32[2,16,768]{2,0,1:T(2,128)S(1)} %maximum_add_fusion.3), channel_id=1, source_target_pairs={{0,256},{16,272},{32,288},{48,304},{64,320},{80,336},{96,352},{112... | collective-permute-start | bytes 294920 | tf_op jit(solution)/shard_map/ppermute | solution.py:11
  155.1 8.5 %copy-start.1 = (f32[2,16,768]{2,1,0:T(8,128)S(1)}, f32[2,16,768]{2,1,0:T(8,128)}, u32[]{:S(2)}) copy-start(f32[2,16,768]{2,1,0:T(8,128)} %param.8) | copy-start | bytes 294916
  155.1 8.5 %copy-start = (f32[2,16,768]{2,1,0:T(8,128)S(1)}, f32[2,16,768]{2,1,0:T(8,128)}, u32[]{:S(2)}) copy-start(f32[2,16,768]{2,1,0:T(8,128)} %param.9) | copy-start | bytes 294916
  155.1 5.1 %collective-permute-start.6 = (f32[2,4,768]{2,1,0:T(4,128)S(1)}, f32[2,4,768]{2,1,0:T(4,128)S(1)}, u32[]{:S(2)}, u32[]{:S(2)}) collective-permute-start(f32[2,4,768]{2,1,0:T(4,128)S(1)} %get-tuple-element.38), channel_id=1, source_target_pairs={{1,0},{2,1},{3,2},{4,3},{5,4},{6,5},{7,6},{8,7},{9,8},{10,9},{11,1... | collective-permute-start | bytes 73736 | tf_op jit(solution)/shard_map/ppermute | solution.py:22
  157.2 6.4 %collective-permute-start.5 = (f32[2,4,768]{2,1,0:T(4,128)S(1)}, f32[2,4,768]{2,1,0:T(4,128)S(1)}, u32[]{:S(2)}, u32[]{:S(2)}) collective-permute-start(f32[2,4,768]{2,1,0:T(4,128)S(1)} %get-tuple-element.37), channel_id=1, source_target_pairs={{0,1},{1,2},{2,3},{3,4},{4,5},{5,6},{6,7},{7,8},{8,9},{9,10},{10,1... | collective-permute-start | bytes 73736 | tf_op jit(solution)/shard_map/ppermute | solution.py:19
  164.4 44.2 %collective-permute-start.8 = (f32[2,4,768]{2,1,0:T(4,128)S(1)}, f32[2,4,768]{2,1,0:T(4,128)S(1)}, u32[]{:S(2)}, u32[]{:S(2)}) collective-permute-start(f32[2,4,768]{2,1,0:T(4,128)S(1)} %get-tuple-element.36), channel_id=1, source_target_pairs={{0,1},{1,2},{2,3},{3,4},{4,5},{5,6},{6,7},{7,8},{8,9},{9,10},{10,1... | collective-permute-start | bytes 73736 | tf_op jit(solution)/shard_map/ppermute | solution.py:19
  166.3 42.3 %collective-permute-start.7 = (f32[2,4,768]{2,1,0:T(4,128)S(1)}, f32[2,4,768]{2,1,0:T(4,128)S(1)}, u32[]{:S(2)}, u32[]{:S(2)}) collective-permute-start(f32[2,4,768]{2,1,0:T(4,128)S(1)} %get-tuple-element.35), channel_id=1, source_target_pairs={{1,0},{2,1},{3,2},{4,3},{5,4},{6,5},{7,6},{8,7},{9,8},{10,9},{11,1... | collective-permute-start | bytes 73736 | tf_op jit(solution)/shard_map/ppermute | solution.py:22
  208.9 8.9 %collective-permute-start.9 = (f32[2,16,768]{2,1,0:T(8,128)S(1)}, f32[2,16,768]{2,1,0:T(8,128)S(1)}, u32[]{:S(2)}, u32[]{:S(2)}) collective-permute-start(f32[2,16,768]{2,1,0:T(8,128)S(1)} %fusion.4), channel_id=1, source_target_pairs={{0,256},{16,272},{32,288},{48,304},{64,320},{80,336},{96,352},{112... | collective-permute-start | bytes 294920 | tf_op jit(solution)/shard_map/ppermute | solution.py:11
  223.9 9.4 %collective-permute-start.10 = (f32[2,16,768]{2,0,1:T(2,128)S(1)}, f32[2,16,768]{2,0,1:T(2,128)S(1)}, u32[]{:S(2)}, u32[]{:S(2)}) collective-permute-start(f32[2,16,768]{2,0,1:T(2,128)S(1)} %convolution_add_fusion.4), channel_id=1, source_target_pairs={{0,128},{16,144},{32,160},{48,176},{64,192},{80,208},{96,224},{112... | collective-permute-start | bytes 294920 | tf_op jit(solution)/shard_map/ppermute | solution.py:11
  240.2 10.4 %collective-permute-start.11 = (f32[2,16,768]{2,0,1:T(2,128)S(1)}, f32[2,16,768]{2,0,1:T(2,128)S(1)}, u32[]{:S(2)}, u32[]{:S(2)}) collective-permute-start(f32[2,16,768]{2,0,1:T(2,128)S(1)} %convolution_add_fusion.3), channel_id=1, source_target_pairs={{0,64},{16,80},{32,96},{48,112},{64,0},{80,16},{96,32},{112,48},{1... | collective-permute-start | bytes 294920 | tf_op jit(solution)/shard_map/ppermute | solution.py:11
  257.4 9.7 %collective-permute-start.12 = (f32[2,16,768]{2,0,1:T(2,128)S(1)}, f32[2,16,768]{2,0,1:T(2,128)S(1)}, u32[]{:S(2)}, u32[]{:S(2)}) collective-permute-start(f32[2,16,768]{2,0,1:T(2,128)S(1)} %convolution_add_fusion.2), channel_id=1, source_target_pairs={{0,32},{16,48},{32,0},{48,16},{64,96},{80,112},{96,64},{112,80},{1... | collective-permute-start | bytes 294920 | tf_op jit(solution)/shard_map/ppermute | solution.py:11
  273.7 8.5 %collective-permute-start.13 = (f32[2,16,768]{2,0,1:T(2,128)S(1)}, f32[2,16,768]{2,0,1:T(2,128)S(1)}, u32[]{:S(2)}, u32[]{:S(2)}) collective-permute-start(f32[2,16,768]{2,0,1:T(2,128)S(1)} %convolution_add_fusion.1), channel_id=1, source_target_pairs={{0,16},{16,0},{32,48},{48,32},{64,80},{80,64},{96,112},{112,96},{1... | collective-permute-start | bytes 294920 | tf_op jit(solution)/shard_map/ppermute | solution.py:11
where the time goes:
time: 292 us; the launch traced here: 289 us
  other arithmetic  106 us (36%)
  between operations  76.9 us (26%)
  starting transfers between devices  53.8 us (18%)
  local copies, waits for them, and re-layouts  42.2 us (14%)
  matrix products  7.3 us (2%)
  waiting for transfers between devices  3.51 us (1%)
    add x23, other arithmetic, shift_taps(): summed + tap_weights[row_index, tap_index] * window[:, offset_in:offset_i...  59.6 us
    another operation x21, other arithmetic, shift_taps(): return jnp.stack(outputs)  43.9 us
    ppermute x10, starting transfers between devices, from_partner(): lax.ppermute(x, axis, [(i, i ^ 1 << apart) for i in range(lax.axis_size(a...  42.5 us
    slice x20, local copies, waits for them, and re-layouts, shift_taps(): begins[row_index]  12.2 us
    slice x15, local copies, waits for them, and re-layouts, shift_taps(): tap_weights[row_index, tap_index] * window[:, offset_in:offset_in + columns]  10.2 us
    dynamic_slice x40, local copies, waits for them, and re-layouts, shift_taps(): lax.dynamic_slice_in_dim(padded[row_index], begins[row_index], columns +...  7.15 us
    ppermute x2, starting transfers between devices, extended(): lax.ppermute(lax.slice_in_dim(block, 0, width, axis=dim), axis, backward)  6.9 us
  transfers between devices with their start and end apart: 14, of which 2 were waited for; matrix products, arithmetic and copies ran while one was open for 30% of the time, Pallas kernels for 0%

commit v1 on v0

v1 whole, which is shorter than its diff:
```python
import functools

import jax
import jax.numpy as jnp
from jax import lax
from jax.experimental import pallas as pl
from jax.experimental.pallas import tpu as pltpu
from jax.sharding import PartitionSpec as P

MESH = pl.DeviceIdType.MESH
F32 = jnp.float32
TAPS = 4
LEVELS = 5
REACH = 4
PLANES = 16
HALF = 16
ROWS = 2 * HALF
CHUNKS = 6
LANES = 128
RING = 8 * LANES
COLUMNS = CHUNKS * LANES
BIAS = (24, 24, 24, 24, 32)
BASE = (128, 104, 80, 56, 32, 0)
UNROLL = 4


def lanes():
    return lax.broadcasted_iota(jnp.int32, (8, LANES), 1)


def places():
    return lax.broadcasted_iota(jnp.int32, (8, LANES), 0) * LANES + lanes()


def ahead(x, k):
    r = pltpu.roll(x, LANES - k, 1)
    return jnp.where(lanes() < LANES - k, r, pltpu.roll(r, 7, 0))


def behind(x, k):
    r = pltpu.roll(x, k, 1)
    return jnp.where(lanes() >= k, r, pltpu.roll(r, 1, 0))


def ahead_by(x, m):
    r = pltpu.roll(x, lax.rem(LANES - m, LANES), 1)
    return jnp.where(lanes() < LANES - m, r, pltpu.roll(r, 7, 0))


def behind_by(x, m):
    r = pltpu.roll(x, m, 1)
    return jnp.where(lanes() >= m, r, pltpu.roll(r, 1, 0))


def within(x, level):
    p = places()
    keep = (p >= BASE[level]) & (p < BASE[level] + COLUMNS)
    return jnp.where(keep, x, 0.0)


def flipped(i, stride):
    return i + stride - 2 * stride * ((i // stride) % 2)


def make_taps(src, taps, shifted):
    def step(i, carry):
        for v in range(2):
            x = src[2 * i + v]
            taps[0, 2 * i + v] = x
            for k in range(1, TAPS):
                taps[k, 2 * i + v] = shifted(x, k)
        return carry

    lax.fori_loop(0, HALF, step, 0, unroll=UNROLL)


def body(
    leaf_hbm, meas_hbm, rayw_hbm, w_s, off_s, src_s, cone_s, res_hbm, upd_hbm,
    leaf_v, meas_v, rayw_v, res_v, upd_v,
    stage, x0, ring_a, ring_b, sib_f, sib_b, taps_a, taps_b, split,
    v_buf, w_buf, meas_t, rayw_t, res_t, cot, g5, back, u_buf,
    in_sem, out_sem, send_sem, recv_sem, sib_sem, halo_send, halo_recv,
):
    d = lax.axis_index("view")
    s = lax.axis_index("slab")
    hi = d // HALF
    lo = d % HALF
    c = s % 2
    slab_to = s - c + hi
    sibling = s + 1 - 2 * c
    other = s - 1 + 2 * c
    has_other = jnp.logical_and(other >= 0, other < 16)
    intra = hi == c

    loads = [
        pltpu.make_async_copy(a, b, in_sem.at[i])
        for i, (a, b) in enumerate(((leaf_hbm, leaf_v), (meas_hbm, meas_v), (rayw_hbm, rayw_v)))
    ]
    for load in loads:
        load.start()

    zero = jnp.zeros((8, LANES), F32)

    def clear(i, carry):
        x0[i] = zero
        g5[i] = zero
        return carry

    lax.fori_loop(0, ROWS, clear, 0, unroll=4)
    for i in range(2 * REACH):
        v_buf[i] = zero
        w_buf[i] = zero
        v_buf[2 * (REACH + PLANES) + i] = zero
        w_buf[2 * (REACH + PLANES) + i] = zero

    barrier = pltpu.get_barrier_semaphore()

    def greet(i, carry):
        to = (lo + i) % HALF

        @pl.when(jnp.logical_not(jnp.logical_and(intra, to == lo)))
        def _():
            pl.semaphore_signal(
                barrier, inc=1, device_id=(HALF * c + to, slab_to), device_id_type=MESH
            )

        return carry

    lax.fori_loop(0, HALF, greet, 0)
    pl.semaphore_signal(barrier, inc=1, device_id=(d, sibling), device_id_type=MESH)

    @pl.when(has_other)
    def _():
        pl.semaphore_signal(barrier, inc=1, device_id=(d, other), device_id_type=MESH)

    def rows_in(dst, src, j0):
        flat = dst.reshape(PLANES * 2 * 8, LANES)
        for v in range(2):
            for h in range(2):
                for j in range(CHUNKS):
                    flat[pl.ds(h * 128 + v * 8 + j0 + j, 8, stride=16), :] = src[
                        v, 8 * h : 8 * h + 8, LANES * j : LANES * (j + 1)
                    ]

    loads[0].wait()
    rows_in(stage, leaf_v, 1)

    pl.semaphore_wait(
        barrier, jnp.where(intra, HALF - 1, HALF) + 1 + jnp.where(has_other, 1, 0)
    )

    def exchange(phase, src, dst, dst_row, first, begin, count):
        def step(n, carry):
            i = begin + (lo + n) % count
            a = src.at[pl.ds(2 * i, 2), pl.ds(first, CHUNKS)]
            b = dst.at[pl.ds(dst_row, 2), pl.ds(first, CHUNKS)]
            own = jnp.logical_and(intra, i == lo)

            @pl.when(own)
            def _():
                pltpu.make_async_copy(a, b, recv_sem.at[phase]).start()

            @pl.when(jnp.logical_not(own))
            def _():
                pltpu.make_async_remote_copy(
                    src_ref=a, dst_ref=b, send_sem=send_sem.at[phase], recv_sem=recv_sem.at[phase],
                    device_id=(HALF * c + i, slab_to), device_id_type=MESH,
                ).start()

            return carry

        lax.fori_loop(0, count, step, 0)

    def arrived(phase, dst, row, first):
        part = dst.at[pl.ds(row, ROWS), pl.ds(first, CHUNKS)]
        pltpu.make_async_copy(part, part, recv_sem.at[phase]).wait()

    def all_sent(phase, src, first):
        @pl.when(intra)
        def _():
            part = src.at[pl.ds(0, ROWS - 2), pl.ds(first, CHUNKS)]
            pltpu.make_async_copy(part, part, send_sem.at[phase]).wait()

        @pl.when(jnp.logical_not(intra))
        def _():
            part = src.at[pl.ds(0, ROWS), pl.ds(first, CHUNKS)]
            pltpu.make_async_copy(part, part, send_sem.at[phase]).wait()

    def to_sibling(n, src, dst):
        return pltpu.make_async_remote_copy(
            src_ref=src, dst_ref=dst, send_sem=sib_sem.at[n, 0], recv_sem=sib_sem.at[n, 1],
            device_id=(d, sibling), device_id_type=MESH,
        )

    exchange(0, stage, x0, 2 * lo, 1, 0, HALF)
    loads[1].wait()
    loads[2].wait()
    rows_in(meas_t, meas_v, 0)
    rows_in(rayw_t, rayw_v, 0)
    arrived(0, x0, 0, 1)

    def forward_term(level, channel, row, base, taps):
        src = base + src_s[level, channel, row]
        z = w_s[level, channel, 0, row] * taps[0, src]
        for k in range(1, TAPS):
            z = z + w_s[level, channel, k, row] * taps[k, src]
        return ahead_by(z, off_s[level, channel, row] + BIAS[level])

    first_row = ROWS * c
    cur = x0
    for level in range(4):
        nxt = (ring_a, ring_b)[level % 2]
        make_taps(cur, taps_a, ahead)

        def step(i, carry, level=level, nxt=nxt):
            far = flipped(i, 2**level)
            for v in range(2):
                row = first_row + 2 * i + v
                y = forward_term(level, 0, row, 2 * i, taps_a) + forward_term(
                    level, 1, row, 2 * far, taps_a
                )
                nxt[2 * i + v] = within(y, level + 1)
            return carry

        lax.fori_loop(0, HALF, step, 0, unroll=UNROLL)
        cur = nxt

    to_sib = to_sibling(0, cur, sib_f)
    to_sib.start()
    make_taps(cur, taps_a, ahead)
    to_sib.wait_recv()
    make_taps(sib_f, taps_b, ahead)

    def last(i, carry):
        for v in range(2):
            row = first_row + 2 * i + v
            y = forward_term(4, 0, row, 2 * i, taps_a) + forward_term(4, 1, row, 2 * i, taps_b)
            split[2 * i + v] = y
        return carry

    lax.fori_loop(0, HALF, last, 0, unroll=UNROLL)

    exchange(1, split, v_buf, 2 * (REACH + lo), 0, 0, HALF)
    arrived(1, v_buf, 2 * REACH, 0)

    low, high = 2 * REACH, 2 * PLANES

    def halo(n, buf):
        up = c == 0
        src = jnp.where(up, high, low)
        dst = jnp.where(up, 0, low + high)
        near = pltpu.make_async_remote_copy(
            src_ref=buf.at[pl.ds(src, 2 * REACH), pl.ds(0, CHUNKS)],
            dst_ref=buf.at[pl.ds(dst, 2 * REACH), pl.ds(0, CHUNKS)],
            send_sem=halo_send.at[n, 0], recv_sem=halo_recv.at[n, 0],
            device_id=(d, sibling), device_id_type=MESH,
        )
        far_src = jnp.where(up, low, high)
        far_dst = jnp.where(up, low + high, 0)
        far = pltpu.make_async_remote_copy(
            src_ref=buf.at[pl.ds(far_src, 2 * REACH), pl.ds(0, CHUNKS)],
            dst_ref=buf.at[pl.ds(far_dst, 2 * REACH), pl.ds(0, CHUNKS)],
            send_sem=halo_send.at[n, 1], recv_sem=halo_recv.at[n, 1],
            device_id=(d, other), device_id_type=MESH,
        )
        return near, far

    def halo_start(pair):
        @pl.when(has_other)
        def _():
            pair[1].start()

        pair[0].start()

    def halo_arrived(pair):
        pair[0].wait_recv()

        @pl.when(has_other)
        def _():
            pair[1].wait_recv()

    def halo_sent(pair):
        pair[0].wait_send()

        @pl.when(has_other)
        def _():
            pair[1].wait_send()

    halo_v = halo(0, v_buf)
    halo_start(halo_v)

    def tilt(z0, z1):
        for v in range(2):
            for z in range(z0, z1):
                acc = cone_s[v, 0] * v_buf[2 * z + v]
                for e in range(1, 2 * REACH + 1):
                    acc = acc + cone_s[v, e] * v_buf[2 * (z + e) + v]
                r = meas_t[2 * z + v] - acc
                res_t[2 * z + v] = r
                w_buf[2 * (z + REACH) + v] = rayw_t[2 * z + v] * r

    def tilt_back(z0, z1):
        for v in range(2):
            for z in range(z0, z1):
                acc = cone_s[v, 0] * w_buf[2 * (z + 2 * REACH) + v]
                for e in range(1, 2 * REACH + 1):
                    acc = acc + cone_s[v, e] * w_buf[2 * (z + 2 * REACH - e) + v]
                cot[2 * z + v] = acc

    tilt(REACH, PLANES - REACH)
    halo_arrived(halo_v)
    tilt(0, REACH)
    tilt(PLANES - REACH, PLANES)
    halo_w = halo(1, w_buf)
    halo_start(halo_w)
    tilt_back(REACH, PLANES - REACH)
    halo_arrived(halo_w)
    tilt_back(0, REACH)
    tilt_back(PLANES - REACH, PLANES)

    exchange(2, cot, g5, 2 * lo, 0, 0, HALF)

    def rows_out(dst, src, j0, plus=None):
        flat = src.reshape(PLANES * 2 * 8, LANES)
        for v in range(2):
            for h in range(2):
                for j in range(CHUNKS):
                    x = flat[pl.ds(h * 128 + v * 8 + j0 + j, 8, stride=16), :]
                    at = (v, slice(8 * h, 8 * h + 8), slice(LANES * j, LANES * (j + 1)))
                    dst[at] = x if plus is None else plus[at] + x

    rows_out(res_v, res_t, 0)
    res_out = pltpu.make_async_copy(res_v, res_hbm, out_sem.at[0])
    res_out.start()
    arrived(2, g5, 0, 0)

    to_sib_b = to_sibling(1, g5, sib_b)
    to_sib_b.start()

    def backward_term(level, channel, row, at, taps):
        z = w_s[level, channel, 0, row] * taps[0, at]
        for k in range(1, TAPS):
            z = z + w_s[level, channel, k, row] * taps[k, at]
        y = behind_by(z, off_s[level, channel, row] + BIAS[level])
        first = src_s[level, channel, row] == 0
        return jnp.where(first, y, 0.0), jnp.where(first, 0.0, y)

    def backward_block(level, i, far, near_row, far_row, near_taps, far_taps, dst):
        sums = [None, None]
        for v in range(2):
            for channel, row, at, taps in (
                (0, near_row + v, 2 * i + v, near_taps),
                (1, far_row + v, 2 * far + v, far_taps),
            ):
                parts = backward_term(level, channel, row, at, taps)
                sums = [p if q is None else q + p for q, p in zip(sums, parts)]
        for v in range(2):
            dst[2 * i + v] = within(sums[v], level)

    make_taps(g5, taps_a, behind)
    to_sib_b.wait_recv()
    make_taps(sib_b, taps_b, behind)
    far_first = ROWS - ROWS * c

    def last_back(i, carry):
        backward_block(
            4, i, i, first_row + 2 * i, far_first + 2 * i, taps_a, taps_b, ring_a_b(4)
        )
        return carry

    def ring_a_b(level):
        return back if level == 0 else (ring_a, ring_b)[level % 2]

    to_sib.wait_send()
    lax.fori_loop(0, HALF, last_back, 0, unroll=UNROLL)
    for level in range(3, -1, -1):
        make_taps(ring_a_b(level + 1), taps_a, behind)

        def step_back(i, carry, level=level):
            far = flipped(i, 2**level)
            backward_block(
                level, i, far, first_row + 2 * i, first_row + 2 * far, taps_a, taps_a,
                ring_a_b(level),
            )
            return carry

        lax.fori_loop(0, HALF, step_back, 0, unroll=UNROLL)

    exchange(3, back, u_buf, 2 * lo, 1, 0, HALF)
    arrived(3, u_buf, 0, 1)
    rows_out(upd_v, u_buf, 1, leaf_v)
    upd_out = pltpu.make_async_copy(upd_v, upd_hbm, out_sem.at[1])
    upd_out.start()
    all_sent(0, stage, 1)
    all_sent(1, split, 0)
    all_sent(2, cot, 0)
    all_sent(3, back, 1)
    to_sib_b.wait_send()
    halo_sent(halo_v)
    halo_sent(halo_w)
    res_out.wait()
    upd_out.wait()


def step(leaf_coeffs, measured, ray_weight, cone_weight, interp_weight, shift_offset, source_view):
    block = leaf_coeffs.shape
    natural = pltpu.VMEM(block, F32)
    rows = pltpu.VMEM((ROWS, 8, LANES), F32)
    taps = pltpu.VMEM((TAPS, ROWS, 8, LANES), F32)
    planes = pltpu.VMEM((2 * (PLANES + 2 * REACH), 8, LANES), F32)
    out = jax.ShapeDtypeStruct(block, F32)
    hbm = pl.BlockSpec(memory_space=pl.ANY)
    smem = pl.BlockSpec(memory_space=pltpu.SMEM)
    return pl.pallas_call(
        body,
        out_shape=(out, out),
        in_specs=[hbm] * 3 + [smem] * 4,
        out_specs=(hbm, hbm),
        scratch_shapes=[natural] * 5
        + [rows] * 6
        + [taps] * 2
        + [rows]
        + [planes] * 2
        + [rows] * 7
        + [
            pltpu.SemaphoreType.DMA((3,)),
            pltpu.SemaphoreType.DMA((2,)),
            pltpu.SemaphoreType.DMA((4,)),
            pltpu.SemaphoreType.DMA((4,)),
            pltpu.SemaphoreType.DMA((2, 2)),
            pltpu.SemaphoreType.DMA((2, 2)),
            pltpu.SemaphoreType.DMA((2, 2)),
        ],
        compiler_params=pltpu.CompilerParams(
            collective_id=0, has_side_effects=True, vmem_limit_bytes=32 << 20
        ),
    )(
        leaf_coeffs, measured, ray_weight,
        jnp.transpose(interp_weight, (0, 1, 3, 2)), shift_offset, source_view, cone_weight,
    )


def solution(mesh):
    in_specs = (
        P("view", "slab", None),
        P("view", "slab", None),
        P("view", "slab", None),
        P("view", None),
        P(),
        P(),
        P(),
    )
    out_specs = (P("view", "slab", None), P("view", "slab", None))
    return jax.shard_map(step, mesh=mesh, in_specs=in_specs, out_specs=out_specs, check_vma=False)
```

time: 292 us -> 68.4 us (0.23)
  the two profiles are of different devices: /device:TPU:34 before, /device:TPU:25 now
where the time goes in v1:
time: 68.4 us; the launch traced here: 68.1 us
  Pallas kernels  60.7 us (89%)
  local copies, waits for them, and re-layouts  6.74 us (10%)
    pallas_call x1, Pallas kernels, step(): pl.pallas_call(body, out_shape=(out, out), in_specs=[hbm] * 3 + [smem] *...  60.7 us
    unnamed x16, local copies, waits for them, and re-layouts  6.74 us

profile of v1, /device:TPU:25, one launch (start us, length us, event | category | flops | bytes accessed | tf_op | source)
XLA Modules:
  0.0 68.1 jit_solution(6434899032227982139)
XLA Ops:
  0.6 0.0 copy-start.6
  0.6 0.7 copy-done.6
  1.3 0.0 copy-start
  1.3 0.9 %copy-done = f32[2,16,768]{2,1,0:T(8,128)S(1)} copy-done((f32[2,16,768]{2,1,0:T(8,128)S(1)}, f32[2,16,768]{2,1,0:T(8,128)}, u32[]{:S(2)}) %copy-start) | copy-done | bytes 98328
  2.2 0.0 copy-start.1
  2.2 0.9 %copy-done.1 = f32[2,16,768]{2,1,0:T(8,128)S(1)} copy-done((f32[2,16,768]{2,1,0:T(8,128)S(1)}, f32[2,16,768]{2,1,0:T(8,128)}, u32[]{:S(2)}) %copy-start.1) | copy-done | bytes 98328
  3.1 0.0 copy-start.2
  3.1 0.9 %copy-done.2 = f32[2,16,768]{2,1,0:T(8,128)S(1)} copy-done((f32[2,16,768]{2,1,0:T(8,128)S(1)}, f32[2,16,768]{2,1,0:T(8,128)}, u32[]{:S(2)}) %copy-start.2) | copy-done | bytes 98328
  4.0 0.0 copy-start.3
  4.0 0.7 %copy-done.3 = f32[5,2,64,4]{2,3,1,0:T(4,128)S(1)} copy-done((f32[5,2,64,4]{2,3,1,0:T(4,128)S(1)}, f32[5,2,64,4]{2,3,1,0:T(4,128)}, u32[]{:S(2)}) %copy-start.3) | copy-done | bytes 10264
  4.7 0.0 copy-start.4
  4.7 0.7 %copy-done.4 = s32[5,2,64]{2,1,0:T(2,128)S(1)} copy-done((s32[5,2,64]{2,1,0:T(2,128)S(1)}, s32[5,2,64]{2,1,0:T(2,128)}, u32[]{:S(2)}) %copy-start.4) | copy-done | bytes 2584
  5.4 0.0 copy-start.5
  5.4 0.7 %copy-done.5 = s32[5,2,64]{2,1,0:T(2,128)S(1)} copy-done((s32[5,2,64]{2,1,0:T(2,128)S(1)}, s32[5,2,64]{2,1,0:T(2,128)}, u32[]{:S(2)}) %copy-start.5) | copy-done | bytes 2584
  6.1 60.7 %shard_map.86 = (f32[2,16,768]{2,1,0:T(8,128)S(1)}, f32[2,16,768]{2,1,0:T(8,128)S(1)}) custom-call(f32[2,16,768]{2,1,0:T(8,128)S(1)} %copy-done, f32[2,16,768]{2,1,0:T(8,128)S(1)} %copy-done.1, f32[2,16,768]{2,1,0:T(8,128)S(1)} %copy-done.2, f32[5,2,4,64]{3,2,1,0:T(4,128)S(1)} %bitcast.1, s32[5,2,64]{2,1,0:T(2,128)S(1)} %copy-done.4, ...), custom_call_target="tpu_custom_call" | custom-call | tf_op jit(solution)/shard_map/pallas_call | solution.py:414
  66.8 0.6 copy.11
  67.5 0.6 copy.12
Async XLA Ops:
  0.6 0.7 copy-start.6
  1.3 0.9 %copy-start = (f32[2,16,768]{2,1,0:T(8,128)S(1)}, f32[2,16,768]{2,1,0:T(8,128)}, u32[]{:S(2)}) copy-start(f32[2,16,768]{2,1,0:T(8,128)} %leaf_hbm.1) | copy-start | bytes 294916
  2.2 0.9 %copy-start.1 = (f32[2,16,768]{2,1,0:T(8,128)S(1)}, f32[2,16,768]{2,1,0:T(8,128)}, u32[]{:S(2)}) copy-start(f32[2,16,768]{2,1,0:T(8,128)} %meas_hbm.1) | copy-start | bytes 294916
  3.1 0.9 %copy-start.2 = (f32[2,16,768]{2,1,0:T(8,128)S(1)}, f32[2,16,768]{2,1,0:T(8,128)}, u32[]{:S(2)}) copy-start(f32[2,16,768]{2,1,0:T(8,128)} %rayw_hbm.1) | copy-start | bytes 294916
  4.0 0.7 %copy-start.3 = (f32[5,2,64,4]{2,3,1,0:T(4,128)S(1)}, f32[5,2,64,4]{2,3,1,0:T(4,128)}, u32[]{:S(2)}) copy-start(f32[5,2,64,4]{2,3,1,0:T(4,128)} %param.11) | copy-start | bytes 30724
  4.7 0.7 %copy-start.4 = (s32[5,2,64]{2,1,0:T(2,128)S(1)}, s32[5,2,64]{2,1,0:T(2,128)}, u32[]{:S(2)}) copy-start(s32[5,2,64]{2,1,0:T(2,128)} %off_s.1) | copy-start | bytes 7684
  5.4 0.7 %copy-start.5 = (s32[5,2,64]{2,1,0:T(2,128)S(1)}, s32[5,2,64]{2,1,0:T(2,128)}, u32[]{:S(2)}) copy-start(s32[5,2,64]{2,1,0:T(2,128)} %src_s.1) | copy-start | bytes 7684

commit v2 on v1

v2 whole, which is shorter than its diff:
```python
import functools

import jax
import jax.numpy as jnp
from jax import lax
from jax.experimental import pallas as pl
from jax.experimental.pallas import tpu as pltpu
from jax.sharding import PartitionSpec as P

MESH = pl.DeviceIdType.MESH
F32 = jnp.float32
TAPS = 4
LEVELS = 5
REACH = 4
EXTRA = 2 * REACH
SLABS = 16
PLANES = 16
HALF = 16
ROWS = 2 * HALF
CHUNKS = 6
LANES = 128
RING = 8 * LANES
COLUMNS = CHUNKS * LANES
BIAS = (24, 24, 24, 24, 32)
BASE = (128, 104, 80, 56, 32, 0)
UNROLL = 16
VMEM_LIMIT = 60 << 20


def lanes():
    return lax.broadcasted_iota(jnp.int32, (8, LANES), 1)


def places():
    return lax.broadcasted_iota(jnp.int32, (8, LANES), 0) * LANES + lanes()


def ahead(x, k):
    r = pltpu.roll(x, LANES - k, 1)
    return jnp.where(lanes() < LANES - k, r, pltpu.roll(r, 7, 0))


def behind(x, k):
    r = pltpu.roll(x, k, 1)
    return jnp.where(lanes() >= k, r, pltpu.roll(r, 1, 0))


def ahead_by(x, m):
    r = pltpu.roll(x, lax.rem(LANES - m, LANES), 1)
    return jnp.where(lanes() < LANES - m, r, pltpu.roll(r, 7, 0))


def behind_by(x, m):
    r = pltpu.roll(x, m, 1)
    return jnp.where(lanes() >= m, r, pltpu.roll(r, 1, 0))


def within(x, level):
    p = places()
    keep = (p >= BASE[level]) & (p < BASE[level] + COLUMNS)
    return jnp.where(keep, x, 0.0)


def flipped(i, stride):
    return i + stride - 2 * stride * ((i // stride) % 2)


def make_taps(src, taps, shifted):
    def step(i, carry):
        for v in range(2):
            x = src[2 * i + v]
            taps[0, 2 * i + v] = x
            for k in range(1, TAPS):
                taps[k, 2 * i + v] = shifted(x, k)
        return carry

    lax.fori_loop(0, HALF, step, 0, unroll=UNROLL)


def body(
    leaf_hbm, meas_hbm, rayw_hbm, w_h, off_h, src_h, cone_h, res_hbm, upd_hbm,
    w_s, off_s, src_s, cone_s,
    leaf_v, meas_v, rayw_v, res_v, upd_v,
    stage, x0, ring_a, ring_b, sib_f, sib_b, taps_a, taps_b, split,
    v_buf, w_buf, mr, res_t, cot, g5, back, u_buf,
    in_sem, out_sem, send_sem, recv_sem, beside_send, sib_sem, halo_send, halo_recv,
):
    d = lax.axis_index("view")
    s = lax.axis_index("slab")
    hi = d // HALF
    lo = d % HALF
    c = s % 2
    slab_to = s - c + hi
    sibling = s + 1 - 2 * c
    other = s - 1 + 2 * c
    has_other = jnp.logical_and(other >= 0, other < 16)
    intra = hi == c

    zero = jnp.zeros((8, LANES), F32)
    for i in range(ROWS):
        x0[i] = zero
        g5[i] = zero

    barrier = pltpu.get_barrier_semaphore()
    for i in range(HALF):
        to = (lo + i + 1) % HALF

        @pl.when(jnp.logical_not(jnp.logical_and(intra, to == lo)))
        def _(to=to):
            pl.semaphore_signal(
                barrier, inc=1, device_id=(HALF * c + to, slab_to), device_id_type=MESH
            )

    pl.semaphore_signal(barrier, inc=1, device_id=(d, sibling), device_id_type=MESH)

    @pl.when(has_other)
    def _():
        pl.semaphore_signal(barrier, inc=1, device_id=(d, other), device_id_type=MESH)

    loads = [
        pltpu.make_async_copy(a, b, in_sem.at[i])
        for i, (a, b) in enumerate(
            (
                (leaf_hbm, leaf_v), (meas_hbm, meas_v), (rayw_hbm, rayw_v),
                (w_h, w_s), (off_h, off_s), (src_h, src_s), (cone_h, cone_s),
            )
        )
    ]
    for load in loads:
        load.start()

    @pl.when(s == 0)
    def _():
        for i in range(2 * EXTRA):
            v_buf[i] = zero
        for i in range(2 * REACH):
            mr[0, i] = zero
            mr[1, i] = zero

    @pl.when(s == SLABS - 1)
    def _():
        for i in range(2 * EXTRA):
            v_buf[2 * (EXTRA + PLANES) + i] = zero
        for i in range(2 * REACH):
            mr[0, 2 * (REACH + PLANES) + i] = zero
            mr[1, 2 * (REACH + PLANES) + i] = zero

    def rows_in(dst, src, j0, plane0=0):
        flat = dst.reshape(dst.shape[0] * 8, LANES)
        for v in range(2):
            for h in range(2):
                for j in range(CHUNKS):
                    flat[pl.ds(16 * plane0 + h * 128 + v * 8 + j0 + j, 8, stride=16), :] = src[
                        v, 8 * h : 8 * h + 8, LANES * j : LANES * (j + 1)
                    ]

    loads[0].wait()
    rows_in(stage, leaf_v, 1)

    pl.semaphore_wait(
        barrier, jnp.where(intra, HALF - 1, HALF) + 1 + jnp.where(has_other, 1, 0)
    )

    def exchange(phase, src, dst, dst_row, first):
        for n in range(HALF):
            i = (lo + n + 1) % HALF
            a = src.at[pl.ds(2 * i, 2), pl.ds(first, CHUNKS)]
            b = dst.at[pl.ds(dst_row, 2), pl.ds(first, CHUNKS)]
            remote = pltpu.make_async_remote_copy(
                src_ref=a, dst_ref=b, send_sem=send_sem.at[phase], recv_sem=recv_sem.at[phase],
                device_id=(HALF * c + i, slab_to), device_id_type=MESH,
            )
            if n < HALF - 1:
                remote.start()
                continue

            @pl.when(intra)
            def _(a=a, b=b):
                pltpu.make_async_copy(a, b, recv_sem.at[phase]).start()

            @pl.when(jnp.logical_not(intra))
            def _(remote=remote):
                remote.start()

    def arrived(phase, dst, row, first, rows=ROWS):
        part = dst.at[pl.ds(row, rows), pl.ds(first, CHUNKS)]
        pltpu.make_async_copy(part, part, recv_sem.at[phase]).wait()

    def all_sent(phase, src, first):
        @pl.when(intra)
        def _():
            part = src.at[pl.ds(0, ROWS - 2), pl.ds(first, CHUNKS)]
            pltpu.make_async_copy(part, part, send_sem.at[phase]).wait()

        @pl.when(jnp.logical_not(intra))
        def _():
            part = src.at[pl.ds(0, ROWS), pl.ds(first, CHUNKS)]
            pltpu.make_async_copy(part, part, send_sem.at[phase]).wait()

    def to_sibling(n, src, dst):
        return pltpu.make_async_remote_copy(
            src_ref=src, dst_ref=dst, send_sem=sib_sem.at[n, 0], recv_sem=sib_sem.at[n, 1],
            device_id=(d, sibling), device_id_type=MESH,
        )

    exchange(0, stage, x0, 2 * lo, 1)
    loads[1].wait()
    loads[2].wait()
    rows_in(mr.at[0], meas_v, 0, REACH)
    rows_in(mr.at[1], rayw_v, 0, REACH)
    low, high, above = 2 * REACH, 2 * PLANES, 2 * (PLANES + REACH)
    up = c == 0

    def edges(n, src, dst, to):
        return pltpu.make_async_remote_copy(
            src_ref=mr.at[:, pl.ds(src, 2 * REACH), pl.ds(0, CHUNKS)],
            dst_ref=mr.at[:, pl.ds(dst, 2 * REACH), pl.ds(0, CHUNKS)],
            send_sem=halo_send.at[n], recv_sem=halo_recv.at[n],
            device_id=(d, to), device_id_type=MESH,
        )

    near = edges(0, jnp.where(up, high, low), jnp.where(up, 0, above), sibling)
    far = edges(1, jnp.where(up, low, high), jnp.where(up, above, 0), other)
    near.start()

    @pl.when(has_other)
    def _():
        far.start()

    for load in loads[3:]:
        load.wait()
    arrived(0, x0, 0, 1)

    def forward_term(level, channel, row, base, taps):
        src = base + src_s[level, channel, row]
        z = w_s[level, channel, 0, row] * taps[0, src]
        for k in range(1, TAPS):
            z = z + w_s[level, channel, k, row] * taps[k, src]
        return ahead_by(z, off_s[level, channel, row] + BIAS[level])

    first_row = ROWS * c
    cur = x0
    for level in range(4):
        nxt = (ring_a, ring_b)[level % 2]
        make_taps(cur, taps_a, ahead)

        def step(i, carry, level=level, nxt=nxt):
            far = flipped(i, 2**level)
            for v in range(2):
                row = first_row + 2 * i + v
                y = forward_term(level, 0, row, 2 * i, taps_a) + forward_term(
                    level, 1, row, 2 * far, taps_a
                )
                nxt[2 * i + v] = within(y, level + 1)
            return carry

        lax.fori_loop(0, HALF, step, 0, unroll=UNROLL)
        cur = nxt

    to_sib = to_sibling(0, cur, sib_f)
    to_sib.start()
    make_taps(cur, taps_a, ahead)

    def own_part(i, carry):
        for v in range(2):
            split[2 * i + v] = forward_term(4, 0, first_row + 2 * i + v, 2 * i, taps_a)
        return carry

    lax.fori_loop(0, HALF, own_part, 0, unroll=UNROLL)
    to_sib.wait_recv()
    make_taps(sib_f, taps_b, ahead)

    def far_part(i, carry):
        for v in range(2):
            split[2 * i + v] += forward_term(4, 1, first_row + 2 * i + v, 2 * i, taps_b)
        return carry

    lax.fori_loop(0, HALF, far_part, 0, unroll=UNROLL)

    exchange(1, split, v_buf, 2 * (EXTRA + lo), 0)
    lower = lo < EXTRA
    slab_beside = jnp.where(lower, slab_to - 1, slab_to + 1)
    has_beside = jnp.logical_and(slab_beside >= 0, slab_beside < SLABS)
    beside_row = 2 * jnp.where(lower, EXTRA + PLANES + lo, EXTRA - PLANES + lo)

    @pl.when(has_beside)
    def _():
        for n in range(HALF):
            i = (lo + n) % HALF
            pltpu.make_async_remote_copy(
                src_ref=split.at[pl.ds(2 * i, 2), pl.ds(0, CHUNKS)],
                dst_ref=v_buf.at[pl.ds(beside_row, 2), pl.ds(0, CHUNKS)],
                send_sem=beside_send, recv_sem=recv_sem.at[1],
                device_id=(HALF * c + i, slab_beside), device_id_type=MESH,
            ).start()

    near.wait_recv()

    @pl.when(has_other)
    def _():
        far.wait_recv()

    inner = jnp.logical_and(s > 0, s < SLABS - 1)

    @pl.when(inner)
    def _():
        arrived(1, v_buf, 0, 0, 2 * (PLANES + 2 * EXTRA))

    @pl.when(jnp.logical_not(inner))
    def _():
        arrived(1, v_buf, 0, 0, 2 * (PLANES + EXTRA))

    for v in range(2):
        for z in range(PLANES + 2 * REACH):
            acc = cone_s[v, 0] * v_buf[2 * z + v]
            for e in range(1, 2 * REACH + 1):
                acc = acc + cone_s[v, e] * v_buf[2 * (z + e) + v]
            r = mr[0, 2 * z + v] - acc
            if REACH <= z < REACH + PLANES:
                res_t[2 * (z - REACH) + v] = r
            w_buf[2 * z + v] = mr[1, 2 * z + v] * r
    for v in range(2):
        for z in range(PLANES):
            acc = cone_s[v, 0] * w_buf[2 * (z + 2 * REACH) + v]
            for e in range(1, 2 * REACH + 1):
                acc = acc + cone_s[v, e] * w_buf[2 * (z + 2 * REACH - e) + v]
            cot[2 * z + v] = acc

    exchange(2, cot, g5, 2 * lo, 0)

    def rows_out(dst, src, j0, plus=None):
        flat = src.reshape(PLANES * 2 * 8, LANES)
        for v in range(2):
            for h in range(2):
                for j in range(CHUNKS):
                    x = flat[pl.ds(h * 128 + v * 8 + j0 + j, 8, stride=16), :]
                    at = (v, slice(8 * h, 8 * h + 8), slice(LANES * j, LANES * (j + 1)))
                    dst[at] = x if plus is None else plus[at] + x

    rows_out(res_v, res_t, 0)
    res_out = pltpu.make_async_copy(res_v, res_hbm, out_sem.at[0])
    res_out.start()
    arrived(2, g5, 0, 0)

    to_sib_b = to_sibling(1, g5, sib_b)
    to_sib_b.start()

    def backward_term(level, channel, row, at, taps):
        z = w_s[level, channel, 0, row] * taps[0, at]
        for k in range(1, TAPS):
            z = z + w_s[level, channel, k, row] * taps[k, at]
        y = behind_by(z, off_s[level, channel, row] + BIAS[level])
        first = src_s[level, channel, row] == 0
        return jnp.where(first, y, 0.0), jnp.where(first, 0.0, y)

    def backward_sums(level, terms, sums=(None, None)):
        for channel, row, at, taps in terms:
            parts = backward_term(level, channel, row, at, taps)
            sums = [p if q is None else q + p for q, p in zip(sums, parts)]
        return sums

    def ring(level):
        return back if level == 0 else (ring_a, ring_b)[level % 2]

    make_taps(g5, taps_a, behind)
    to_sib.wait_send()
    far_first = ROWS - ROWS * c

    def own_back(i, carry):
        sums = backward_sums(
            4, [(0, first_row + 2 * i + v, 2 * i + v, taps_a) for v in range(2)]
        )
        for v in range(2):
            ring(4)[2 * i + v] = sums[v]
        return carry

    lax.fori_loop(0, HALF, own_back, 0, unroll=UNROLL)
    to_sib_b.wait_recv()
    make_taps(sib_b, taps_b, behind)

    def far_back(i, carry):
        sums = backward_sums(
            4,
            [(1, far_first + 2 * i + v, 2 * i + v, taps_b) for v in range(2)],
            [ring(4)[2 * i + v] for v in range(2)],
        )
        for v in range(2):
            ring(4)[2 * i + v] = within(sums[v], 4)
        return carry

    lax.fori_loop(0, HALF, far_back, 0, unroll=UNROLL)
    for level in range(3, -1, -1):
        make_taps(ring(level + 1), taps_a, behind)

        def step_back(i, carry, level=level):
            far = flipped(i, 2**level)
            sums = backward_sums(
                level,
                [(0, first_row + 2 * i + v, 2 * i + v, taps_a) for v in range(2)]
                + [(1, first_row + 2 * far + v, 2 * far + v, taps_a) for v in range(2)],
            )
            for v in range(2):
                ring(level)[2 * i + v] = within(sums[v], level)
            return carry

        lax.fori_loop(0, HALF, step_back, 0, unroll=UNROLL)

    exchange(3, back, u_buf, 2 * lo, 1)
    arrived(3, u_buf, 0, 1)
    rows_out(upd_v, u_buf, 1, leaf_v)
    upd_out = pltpu.make_async_copy(upd_v, upd_hbm, out_sem.at[1])
    upd_out.start()
    all_sent(0, stage, 1)
    all_sent(1, split, 0)
    all_sent(2, cot, 0)
    all_sent(3, back, 1)
    to_sib_b.wait_send()
    near.wait_send()

    @pl.when(has_other)
    def _():
        far.wait_send()

    @pl.when(has_beside)
    def _():
        part = split.at[pl.ds(0, ROWS), pl.ds(0, CHUNKS)]
        pltpu.make_async_copy(part, part, beside_send).wait()

    res_out.wait()
    upd_out.wait()


def step(leaf_coeffs, measured, ray_weight, cone_weight, interp_weight, shift_offset, source_view):
    block = leaf_coeffs.shape
    natural = pltpu.VMEM(block, F32)
    rows = pltpu.VMEM((ROWS, 8, LANES), F32)
    taps = pltpu.VMEM((TAPS, ROWS, 8, LANES), F32)
    planes_v = pltpu.VMEM((2 * (PLANES + 2 * EXTRA), 8, LANES), F32)
    planes_w = pltpu.VMEM((2 * (PLANES + 2 * REACH), 8, LANES), F32)
    planes_mr = pltpu.VMEM((2, 2 * (PLANES + 2 * REACH), 8, LANES), F32)
    out = jax.ShapeDtypeStruct(block, F32)
    hbm = pl.BlockSpec(memory_space=pl.ANY)
    return pl.pallas_call(
        body,
        out_shape=(out, out),
        in_specs=[hbm] * 7,
        out_specs=(hbm, hbm),
        scratch_shapes=[
            pltpu.SMEM((LEVELS, 2, TAPS, 64), F32),
            pltpu.SMEM((LEVELS, 2, 64), jnp.int32),
            pltpu.SMEM((LEVELS, 2, 64), jnp.int32),
            pltpu.SMEM((2, 2 * REACH + 1), F32),
        ]
        + [natural] * 5
        + [rows] * 6
        + [taps] * 2
        + [rows]
        + [planes_v, planes_w, planes_mr]
        + [rows] * 5
        + [
            pltpu.SemaphoreType.DMA((7,)),
            pltpu.SemaphoreType.DMA((2,)),
            pltpu.SemaphoreType.DMA((4,)),
            pltpu.SemaphoreType.DMA((4,)),
            pltpu.SemaphoreType.DMA,
            pltpu.SemaphoreType.DMA((2, 2)),
            pltpu.SemaphoreType.DMA((2,)),
            pltpu.SemaphoreType.DMA((2,)),
        ],
        compiler_params=pltpu.CompilerParams(
            collective_id=0, has_side_effects=True, vmem_limit_bytes=VMEM_LIMIT
        ),
    )(
        leaf_coeffs, measured, ray_weight,
        jnp.transpose(interp_weight, (0, 1, 3, 2)), shift_offset, source_view, cone_weight,
    )


def solution(mesh):
    in_specs = (
        P("view", "slab", None),
        P("view", "slab", None),
        P("view", "slab", None),
        P("view", None),
        P(),
        P(),
        P(),
    )
    out_specs = (P("view", "slab", None), P("view", "slab", None))
    return jax.shard_map(step, mesh=mesh, in_specs=in_specs, out_specs=out_specs, check_vma=False)
```

time: 68.4 us -> 51.8 us (0.76)
  Pallas kernels: 60.7 us -> 48.7 us
  local copies, waits for them, and re-layouts: 6.74 us -> 2.22 us
    pallas_call x1, Pallas kernels: 60.7 us -> 48.7 us  [step(): pl.pallas_call(body, out_shape=(out, out), in_specs=[hbm] * 7, out_specs=...]
    unnamed x16 -> x4, local copies, waits for them, and re-layouts: 6.74 us -> 2.22 us
where the time goes in v2:
time: 51.8 us; the launch traced here: 51.6 us
  Pallas kernels  48.7 us (94%)
  local copies, waits for them, and re-layouts  2.22 us (4%)
  between operations  0.65 us (1%)
    pallas_call x1, Pallas kernels, step(): pl.pallas_call(body, out_shape=(out, out), in_specs=[hbm] * 7, out_specs=...  48.7 us
    unnamed x4, local copies, waits for them, and re-layouts  2.22 us

profile of v2, /device:TPU:25, one launch (start us, length us, event | category | flops | bytes accessed | tf_op | source)
XLA Modules:
  0.0 51.6 jit_solution(15870117943474308137)
XLA Ops:
  0.6 48.7 %shard_map.86 = (f32[2,16,768]{2,1,0:T(8,128)}, f32[2,16,768]{2,1,0:T(8,128)}) custom-call(f32[2,16,768]{2,1,0:T(8,128)} %leaf_hbm.1, f32[2,16,768]{2,1,0:T(8,128)} %meas_hbm.1, f32[2,16,768]{2,1,0:T(8,128)} %rayw_hbm.1, f32[5,2,4,64]{3,2,1,0:T(4,128)} %bitcast.1, s32[5,2,64]{2,1,0:T(2,128)} %off_h.1, s32[5,2,64]{2,1,0:T(2,128)} %src_h.1, f32[2,9]{1,0:T(2,128)} %cone_h.1), custom_call_target="tpu_custom_call" | custom-call | tf_op jit(solution)/shard_map/pallas_call | solution.py:443
  49.3 0.0 copy-start
  49.4 1.6 %copy.11 = f32[2,16,768]{2,1,0:T(8,128)} copy(f32[2,16,768]{2,1,0:T(8,128)} %get-tuple-element.4) | data formatting | bytes 196608
  50.9 0.0 copy-done
  50.9 0.6 %copy.12 = f32[2,16,768]{2,1,0:T(8,128)} copy(f32[2,16,768]{2,1,0:T(8,128)S(1)} %copy-done) | data formatting | bytes 196608
Async XLA Ops:
  49.3 1.6 %copy-start = (f32[2,16,768]{2,1,0:T(8,128)S(1)}, f32[2,16,768]{2,1,0:T(8,128)}, u32[]{:S(2)}) copy-start(f32[2,16,768]{2,1,0:T(8,128)} %get-tuple-element.5) | copy-start | bytes 294916

commit v3 on v2

--- a/solution.py
+++ b/solution.py
@@ -24,7 +24,8 @@
 BIAS = (24, 24, 24, 24, 32)
 BASE = (128, 104, 80, 56, 32, 0)
 UNROLL = 16
-VMEM_LIMIT = 60 << 20
+FAR_FIRST = tuple((a, b) for b in (4, 3, 5, 2, 6, 1, 7, 0) for a in (1, 0))
+VMEM_LIMIT = 24 << 20
 
 
 def lanes():
@@ -43,16 +44,6 @@
 def behind(x, k):
     r = pltpu.roll(x, k, 1)
     return jnp.where(lanes() >= k, r, pltpu.roll(r, 1, 0))
-
-
-def ahead_by(x, m):
-    r = pltpu.roll(x, lax.rem(LANES - m, LANES), 1)
-    return jnp.where(lanes() < LANES - m, r, pltpu.roll(r, 7, 0))
-
-
-def behind_by(x, m):
-    r = pltpu.roll(x, m, 1)
-    return jnp.where(lanes() >= m, r, pltpu.roll(r, 1, 0))
 
 
 def within(x, level):
@@ -78,12 +69,13 @@
 
 
 def body(
-    leaf_hbm, meas_hbm, rayw_hbm, w_h, off_h, src_h, cone_h, res_hbm, upd_hbm,
+    leaf_hbm, meas_hbm, rayw_hbm, w_h, off_h, src_h, cone_h, res_v, upd_v,
     w_s, off_s, src_s, cone_s,
-    leaf_v, meas_v, rayw_v, res_v, upd_v,
+    leaf_v, meas_v, rayw_v,
     stage, x0, ring_a, ring_b, sib_f, sib_b, taps_a, taps_b, split,
+    w_t, m_t, s_t, w_far, m_far, s_far,
     v_buf, w_buf, mr, res_t, cot, g5, back, u_buf,
-    in_sem, out_sem, send_sem, recv_sem, beside_send, sib_sem, halo_send, halo_recv,
+    in_sem, send_sem, recv_sem, beside_send, sib_sem, halo_send, halo_recv,
 ):
     d = lax.axis_index("view")
     s = lax.axis_index("slab")
@@ -97,19 +89,23 @@
     intra = hi == c
 
     zero = jnp.zeros((8, LANES), F32)
-    for i in range(ROWS):
-        x0[i] = zero
-        g5[i] = zero
-
     barrier = pltpu.get_barrier_semaphore()
-    for i in range(HALF):
-        to = (lo + i + 1) % HALF
-
-        @pl.when(jnp.logical_not(jnp.logical_and(intra, to == lo)))
-        def _(to=to):
-            pl.semaphore_signal(
-                barrier, inc=1, device_id=(HALF * c + to, slab_to), device_id_type=MESH
-            )
+    across, along = d // 8, d % 8
+
+    def nth(n):
+        a, b = FAR_FIRST[n]
+        return 8 * ((across + a) % 2) + (along + b) % 8
+
+    for n in range(HALF - 1):
+        pl.semaphore_signal(
+            barrier, inc=1, device_id=(HALF * c + nth(n), slab_to), device_id_type=MESH
+        )
+
+    @pl.when(jnp.logical_not(intra))
+    def _():
+        pl.semaphore_signal(
+            barrier, inc=1, device_id=(HALF * c + lo, slab_to), device_id_type=MESH
+        )
 
     pl.semaphore_signal(barrier, inc=1, device_id=(d, sibling), device_id_type=MESH)
 
@@ -129,6 +125,11 @@
     for load in loads:
         load.start()
 
+    for i in range(ROWS):
+        x0[i, 0:1] = zero[0:1]
+        x0[i, 7:8] = zero[0:1]
+        g5[i, 6:8] = zero[0:2]
+
     @pl.when(s == 0)
     def _():
         for i in range(2 * EXTRA):
@@ -163,7 +164,7 @@
 
     def exchange(phase, src, dst, dst_row, first):
         for n in range(HALF):
-            i = (lo + n + 1) % HALF
+            i = nth(n)
             a = src.at[pl.ds(2 * i, 2), pl.ds(first, CHUNKS)]
             b = dst.at[pl.ds(dst_row, 2), pl.ds(first, CHUNKS)]
             remote = pltpu.make_async_remote_copy(
@@ -229,16 +230,38 @@
 
     for load in loads[3:]:
         load.wait()
+    first_row = ROWS * c
+    far_first = ROWS - ROWS * c
+
+    def spread(level, channel, row, at, w, m, sel):
+        for k in range(TAPS):
+            w[TAPS * at + k] = jnp.full((8, LANES), w_s[level, channel, k, row], F32)
+        m[at] = jnp.full((8, LANES), off_s[level, channel, row], jnp.int32)
+        sel[at] = jnp.full((8, LANES), src_s[level, channel, row], jnp.int32).astype(F32)
+
+    def spread_rows(r, carry):
+        for level in range(LEVELS):
+            for channel in range(2):
+                spread(
+                    level, channel, first_row + r, ROWS * (2 * level + channel) + r, w_t, m_t, s_t
+                )
+        spread(LEVELS - 1, 1, far_first + r, r, w_far, m_far, s_far)
+        return carry
+
+    lax.fori_loop(0, ROWS, spread_rows, 0)
     arrived(0, x0, 0, 1)
 
-    def forward_term(level, channel, row, base, taps):
+    def forward_term(level, channel, r, base, taps):
+        row, at = first_row + r, ROWS * (2 * level + channel) + r
         src = base + src_s[level, channel, row]
-        z = w_s[level, channel, 0, row] * taps[0, src]
+        z = w_t[TAPS * at] * taps[0, src]
         for k in range(1, TAPS):
-            z = z + w_s[level, channel, k, row] * taps[k, src]
-        return ahead_by(z, off_s[level, channel, row] + BIAS[level])
-
-    first_row = ROWS * c
+            z = z + w_t[TAPS * at + k] * taps[k, src]
+        by = off_s[level, channel, row] + BIAS[level]
+        turned = pltpu.roll(z, lax.rem(LANES - by, LANES), 1)
+        keep = (LANES - 1 - BIAS[level]) - lanes() >= m_t[at]
+        return jnp.where(keep, turned, pltpu.roll(turned, 7, 0))
+
     cur = x0
     for level in range(4):
         nxt = (ring_a, ring_b)[level % 2]
@@ -247,9 +270,9 @@
         def step(i, carry, level=level, nxt=nxt):
             far = flipped(i, 2**level)
             for v in range(2):
-                row = first_row + 2 * i + v
-                y = forward_term(level, 0, row, 2 * i, taps_a) + forward_term(
-                    level, 1, row, 2 * far, taps_a
+                r = 2 * i + v
+                y = forward_term(level, 0, r, 2 * i, taps_a) + forward_term(
+                    level, 1, r, 2 * far, taps_a
                 )
                 nxt[2 * i + v] = within(y, level + 1)
             return carry
@@ -263,7 +286,7 @@
 
     def own_part(i, carry):
         for v in range(2):
-            split[2 * i + v] = forward_term(4, 0, first_row + 2 * i + v, 2 * i, taps_a)
+            split[2 * i + v] = forward_term(4, 0, 2 * i + v, 2 * i, taps_a)
         return carry
 
     lax.fori_loop(0, HALF, own_part, 0, unroll=UNROLL)
@@ -272,12 +295,11 @@
 
     def far_part(i, carry):
         for v in range(2):
-            split[2 * i + v] += forward_term(4, 1, first_row + 2 * i + v, 2 * i, taps_b)
+            split[2 * i + v] += forward_term(4, 1, 2 * i + v, 2 * i, taps_b)
         return carry
 
     lax.fori_loop(0, HALF, far_part, 0, unroll=UNROLL)
 
-    exchange(1, split, v_buf, 2 * (EXTRA + lo), 0)
     lower = lo < EXTRA
     slab_beside = jnp.where(lower, slab_to - 1, slab_to + 1)
     has_beside = jnp.logical_and(slab_beside >= 0, slab_beside < SLABS)
@@ -286,7 +308,7 @@
     @pl.when(has_beside)
     def _():
         for n in range(HALF):
-            i = (lo + n) % HALF
+            i = nth(n)
             pltpu.make_async_remote_copy(
                 src_ref=split.at[pl.ds(2 * i, 2), pl.ds(0, CHUNKS)],
                 dst_ref=v_buf.at[pl.ds(beside_row, 2), pl.ds(0, CHUNKS)],
@@ -294,6 +316,7 @@
                 device_id=(HALF * c + i, slab_beside), device_id_type=MESH,
             ).start()
 
+    exchange(1, split, v_buf, 2 * (EXTRA + lo), 0)
     near.wait_recv()
 
     @pl.when(has_other)
@@ -338,24 +361,27 @@
                     dst[at] = x if plus is None else plus[at] + x
 
     rows_out(res_v, res_t, 0)
-    res_out = pltpu.make_async_copy(res_v, res_hbm, out_sem.at[0])
-    res_out.start()
     arrived(2, g5, 0, 0)
 
     to_sib_b = to_sibling(1, g5, sib_b)
     to_sib_b.start()
 
-    def backward_term(level, channel, row, at, taps):
-        z = w_s[level, channel, 0, row] * taps[0, at]
+    def backward_term(level, channel, r, taps, tables=None):
+        w, m, sel = tables or (w_t, m_t, s_t)
+        at = r if tables else ROWS * (2 * level + channel) + r
+        row = (far_first if tables else first_row) + r
+        z = w[TAPS * at] * taps[0, r]
         for k in range(1, TAPS):
-            z = z + w_s[level, channel, k, row] * taps[k, at]
-        y = behind_by(z, off_s[level, channel, row] + BIAS[level])
-        first = src_s[level, channel, row] == 0
-        return jnp.where(first, y, 0.0), jnp.where(first, 0.0, y)
+            z = z + w[TAPS * at + k] * taps[k, r]
+        by = off_s[level, channel, row] + BIAS[level]
+        turned = pltpu.roll(z, by, 1)
+        y = jnp.where(lanes() - BIAS[level] >= m[at], turned, pltpu.roll(turned, 1, 0))
+        second = y * sel[at]
+        return y - second, second
 
     def backward_sums(level, terms, sums=(None, None)):
-        for channel, row, at, taps in terms:
-            parts = backward_term(level, channel, row, at, taps)
+        for term in terms:
+            parts = backward_term(level, *term)
             sums = [p if q is None else q + p for q, p in zip(sums, parts)]
         return sums
 
@@ -364,11 +390,10 @@
 
     make_taps(g5, taps_a, behind)
     to_sib.wait_send()
-    far_first = ROWS - ROWS * c
 
     def own_back(i, carry):
         sums = backward_sums(
-            4, [(0, first_row + 2 * i + v, 2 * i + v, taps_a) for v in range(2)]
+            4, [(0, 2 * i + v, taps_a) for v in range(2)]
         )
         for v in range(2):
             ring(4)[2 * i + v] = sums[v]
@@ -381,7 +406,7 @@
     def far_back(i, carry):
         sums = backward_sums(
             4,
-            [(1, far_first + 2 * i + v, 2 * i + v, taps_b) for v in range(2)],
+            [(1, 2 * i + v, taps_b, (w_far, m_far, s_far)) for v in range(2)],
             [ring(4)[2 * i + v] for v in range(2)],
         )
         for v in range(2):
@@ -396,8 +421,8 @@
             far = flipped(i, 2**level)
             sums = backward_sums(
                 level,
-                [(0, first_row + 2 * i + v, 2 * i + v, taps_a) for v in range(2)]
-                + [(1, first_row + 2 * far + v, 2 * far + v, taps_a) for v in range(2)],
+                [(0, 2 * i + v, taps_a) for v in range(2)]
+                + [(1, 2 * far + v, taps_a) for v in range(2)],
             )
             for v in range(2):
                 ring(level)[2 * i + v] = within(sums[v], level)
@@ -408,8 +433,6 @@
     exchange(3, back, u_buf, 2 * lo, 1)
     arrived(3, u_buf, 0, 1)
     rows_out(upd_v, u_buf, 1, leaf_v)
-    upd_out = pltpu.make_async_copy(upd_v, upd_hbm, out_sem.at[1])
-    upd_out.start()
     all_sent(0, stage, 1)
     all_sent(1, split, 0)
     all_sent(2, cot, 0)
@@ -425,9 +448,6 @@
     def _():
         part = split.at[pl.ds(0, ROWS), pl.ds(0, CHUNKS)]
         pltpu.make_async_copy(part, part, beside_send).wait()
-
-    res_out.wait()
-    upd_out.wait()
 
 
 def step(leaf_coeffs, measured, ray_weight, cone_weight, interp_weight, shift_offset, source_view):
@@ -440,26 +460,37 @@
     planes_mr = pltpu.VMEM((2, 2 * (PLANES + 2 * REACH), 8, LANES), F32)
     out = jax.ShapeDtypeStruct(block, F32)
     hbm = pl.BlockSpec(memory_space=pl.ANY)
-    return pl.pallas_call(
+    operands = (
+        leaf_coeffs, measured, ray_weight,
+        jnp.transpose(interp_weight, (0, 1, 3, 2)), shift_offset, source_view, cone_weight,
+    )
+    res, upd = pl.pallas_call(
         body,
         out_shape=(out, out),
         in_specs=[hbm] * 7,
-        out_specs=(hbm, hbm),
+        out_specs=(pl.BlockSpec(memory_space=pltpu.VMEM),) * 2,
         scratch_shapes=[
             pltpu.SMEM((LEVELS, 2, TAPS, 64), F32),
             pltpu.SMEM((LEVELS, 2, 64), jnp.int32),
             pltpu.SMEM((LEVELS, 2, 64), jnp.int32),
             pltpu.SMEM((2, 2 * REACH + 1), F32),
         ]
-        + [natural] * 5
+        + [natural] * 3
         + [rows] * 6
         + [taps] * 2
         + [rows]
+        + [
+            pltpu.VMEM((2 * LEVELS * ROWS * TAPS, 8, LANES), F32),
+            pltpu.VMEM((2 * LEVELS * ROWS, 8, LANES), jnp.int32),
+            pltpu.VMEM((2 * LEVELS * ROWS, 8, LANES), F32),
+            pltpu.VMEM((ROWS * TAPS, 8, LANES), F32),
+            pltpu.VMEM((ROWS, 8, LANES), jnp.int32),
+            pltpu.VMEM((ROWS, 8, LANES), F32),
+        ]
         + [planes_v, planes_w, planes_mr]
         + [rows] * 5
         + [
             pltpu.SemaphoreType.DMA((7,)),
-            pltpu.SemaphoreType.DMA((2,)),
             pltpu.SemaphoreType.DMA((4,)),
             pltpu.SemaphoreType.DMA((4,)),
             pltpu.SemaphoreType.DMA,
@@ -470,10 +501,26 @@
         compiler_params=pltpu.CompilerParams(
             collective_id=0, has_side_effects=True, vmem_limit_bytes=VMEM_LIMIT
         ),
-    )(
-        leaf_coeffs, measured, ray_weight,
-        jnp.transpose(interp_weight, (0, 1, 3, 2)), shift_offset, source_view, cone_weight,
-    )
+    )(*(pltpu.with_memory_space_constraint(x, pltpu.HBM) for x in operands))
+    return pl.pallas_call(
+        finish,
+        out_shape=(out, out),
+        in_specs=[hbm] * 2,
+        out_specs=(hbm, hbm),
+        scratch_shapes=[pltpu.SemaphoreType.DMA((2,))],
+        compiler_params=pltpu.CompilerParams(vmem_limit_bytes=1 << 20),
+    )(res, upd)
+
+
+def finish(res, upd, res_hbm, upd_hbm, sem):
+    copies = [
+        pltpu.make_async_copy(a, b, sem.at[i])
+        for i, (a, b) in enumerate(((res, res_hbm), (upd, upd_hbm)))
+    ]
+    for copy in copies:
+        copy.start()
+    for copy in copies:
+        copy.wait()
 
 
 def solution(mesh):

time: 51.8 us -> 44.8 us (0.86)
  the two profiles are of different devices: /device:TPU:25 before, /device:TPU:1 now
where the time goes in v3:
time: 44.8 us; the launch traced here: 44.6 us
  Pallas kernels  44 us (98%)
  between operations  0.64 us (1%)
    pallas_call x1, Pallas kernels, step(): pl.pallas_call(body, out_shape=(out, out), in_specs=[hbm] * 7, out_specs=...  43.3 us

profile of v3, /device:TPU:1, one launch (start us, length us, event | category | flops | bytes accessed | tf_op | source)
XLA Modules:
  0.0 44.6 jit_solution(1550852551504336240)
XLA Ops:
  0.6 43.3 %shard_map.86 = (f32[2,16,768]{2,1,0:T(8,128)S(1)}, f32[2,16,768]{2,1,0:T(8,128)S(1)}) custom-call(f32[2,16,768]{2,1,0:T(8,128)} %leaf_hbm.1, f32[2,16,768]{2,1,0:T(8,128)} %meas_hbm.1, f32[2,16,768]{2,1,0:T(8,128)} %rayw_hbm.1, f32[5,2,4,64]{3,2,1,0:T(4,128)} %bitcast.1, s32[5,2,64]{2,1,0:T(2,128)} %off_h.1, s32[5,2,64]{2,1,0:T(2,128)} %src_h.1, f32[2,9]{1,0:T(2,128)} %cone_h.1), custom_call_target="tpu_custom_call" | custom-call | tf_op jit(solution)/shard_map/pallas_call | solution.py:467
  43.9 0.7 %shard_map.87 = (f32[2,16,768]{2,1,0:T(8,128)}, f32[2,16,768]{2,1,0:T(8,128)}) custom-call(f32[2,16,768]{2,1,0:T(8,128)S(1)} %get-tuple-element.4.res, f32[2,16,768]{2,1,0:T(8,128)S(1)} %get-tuple-element.5.upd), custom_call_target="tpu_custom_call" | custom-call | tf_op jit(solution)/shard_map/pallas_call | solution.py:505

commit v4 on v3

--- a/solution.py
+++ b/solution.py
@@ -37,13 +37,11 @@
 
 
 def ahead(x, k):
-    r = pltpu.roll(x, LANES - k, 1)
-    return jnp.where(lanes() < LANES - k, r, pltpu.roll(r, 7, 0))
+    return pltpu.roll(jnp.where(lanes() >= k, x, pltpu.roll(x, 7, 0)), LANES - k, 1)
 
 
 def behind(x, k):
-    r = pltpu.roll(x, k, 1)
-    return jnp.where(lanes() >= k, r, pltpu.roll(r, 1, 0))
+    return pltpu.roll(jnp.where(lanes() < LANES - k, x, pltpu.roll(x, 1, 0)), k, 1)
 
 
 def within(x, level):
@@ -260,7 +258,13 @@
         by = off_s[level, channel, row] + BIAS[level]
         turned = pltpu.roll(z, lax.rem(LANES - by, LANES), 1)
         keep = (LANES - 1 - BIAS[level]) - lanes() >= m_t[at]
-        return jnp.where(keep, turned, pltpu.roll(turned, 7, 0))
+        return jnp.where(keep, turned, 0.0), jnp.where(keep, 0.0, turned)
+
+    def forward_row(terms):
+        here, above = terms[0]
+        for a, b in terms[1:]:
+            here, above = here + a, above + b
+        return here + pltpu.roll(above, 7, 0)
 
     cur = x0
     for level in range(4):
@@ -271,9 +275,9 @@
             far = flipped(i, 2**level)
             for v in range(2):
                 r = 2 * i + v
-                y = forward_term(level, 0, r, 2 * i, taps_a) + forward_term(
+                y = forward_row([forward_term(level, 0, r, 2 * i, taps_a), forward_term(
                     level, 1, r, 2 * far, taps_a
-                )
+                )])
                 nxt[2 * i + v] = within(y, level + 1)
             return carry
 
@@ -286,7 +290,7 @@
 
     def own_part(i, carry):
         for v in range(2):
-            split[2 * i + v] = forward_term(4, 0, 2 * i + v, 2 * i, taps_a)
+            split[2 * i + v] = forward_row([forward_term(4, 0, 2 * i + v, 2 * i, taps_a)])
         return carry
 
     lax.fori_loop(0, HALF, own_part, 0, unroll=UNROLL)
@@ -295,7 +299,7 @@
 
     def far_part(i, carry):
         for v in range(2):
-            split[2 * i + v] += forward_term(4, 1, 2 * i + v, 2 * i, taps_b)
+            split[2 * i + v] += forward_row([forward_term(4, 1, 2 * i + v, 2 * i, taps_b)])
         return carry
 
     lax.fori_loop(0, HALF, far_part, 0, unroll=UNROLL)
@@ -304,6 +308,8 @@
     slab_beside = jnp.where(lower, slab_to - 1, slab_to + 1)
     has_beside = jnp.logical_and(slab_beside >= 0, slab_beside < SLABS)
     beside_row = 2 * jnp.where(lower, EXTRA + PLANES + lo, EXTRA - PLANES + lo)
+
+    exchange(1, split, v_buf, 2 * (EXTRA + lo), 0)
 
     @pl.when(has_beside)
     def _():
@@ -316,7 +322,6 @@
                 device_id=(HALF * c + i, slab_beside), device_id_type=MESH,
             ).start()
 
-    exchange(1, split, v_buf, 2 * (EXTRA + lo), 0)
     near.wait_recv()
 
     @pl.when(has_other)
@@ -363,7 +368,7 @@
     rows_out(res_v, res_t, 0)
     arrived(2, g5, 0, 0)
 
-    to_sib_b = to_sibling(1, g5, sib_b)
+    to_sib_b = to_sibling(1, g5.at[pl.ds(0, ROWS)], sib_b)
     to_sib_b.start()
 
     def backward_term(level, channel, r, taps, tables=None):
@@ -454,6 +459,7 @@
     block = leaf_coeffs.shape
     natural = pltpu.VMEM(block, F32)
     rows = pltpu.VMEM((ROWS, 8, LANES), F32)
+    rows_more = pltpu.VMEM((ROWS + 1, 8, LANES), F32)
     taps = pltpu.VMEM((TAPS, ROWS, 8, LANES), F32)
     planes_v = pltpu.VMEM((2 * (PLANES + 2 * EXTRA), 8, LANES), F32)
     planes_w = pltpu.VMEM((2 * (PLANES + 2 * REACH), 8, LANES), F32)
@@ -476,7 +482,8 @@
             pltpu.SMEM((2, 2 * REACH + 1), F32),
         ]
         + [natural] * 3
-        + [rows] * 6
+        + [rows, rows_more]
+        + [rows] * 4
         + [taps] * 2
         + [rows]
         + [
@@ -488,7 +495,9 @@
             pltpu.VMEM((ROWS, 8, LANES), F32),
         ]
         + [planes_v, planes_w, planes_mr]
-        + [rows] * 5
+        + [rows] * 2
+        + [rows_more]
+        + [rows] * 2
         + [
             pltpu.SemaphoreType.DMA((7,)),
             pltpu.SemaphoreType.DMA((4,)),

time: 44.8 us -> 44.7 us (level)
  the two profiles are of different devices: /device:TPU:1 before, /device:TPU:25 now
where the time goes in v4:
time: 44.7 us; the launch traced here: 44.5 us
  Pallas kernels  43.9 us (98%)
  between operations  0.64 us (1%)
    pallas_call x1, Pallas kernels, step(): pl.pallas_call(body, out_shape=(out, out), in_specs=[hbm] * 7, out_specs=...  43.2 us

profile of v4, /device:TPU:25, one launch (start us, length us, event | category | flops | bytes accessed | tf_op | source)
XLA Modules:
  0.0 44.5 jit_solution(8294232507198577466)
XLA Ops:
  0.6 43.2 %shard_map.86 = (f32[2,16,768]{2,1,0:T(8,128)S(1)}, f32[2,16,768]{2,1,0:T(8,128)S(1)}) custom-call(f32[2,16,768]{2,1,0:T(8,128)} %leaf_hbm.1, f32[2,16,768]{2,1,0:T(8,128)} %meas_hbm.1, f32[2,16,768]{2,1,0:T(8,128)} %rayw_hbm.1, f32[5,2,4,64]{3,2,1,0:T(4,128)} %bitcast.1, s32[5,2,64]{2,1,0:T(2,128)} %off_h.1, s32[5,2,64]{2,1,0:T(2,128)} %src_h.1, f32[2,9]{1,0:T(2,128)} %cone_h.1), custom_call_target="tpu_custom_call" | custom-call | tf_op jit(solution)/shard_map/pallas_call | solution.py:473
  43.9 0.7 %shard_map.87 = (f32[2,16,768]{2,1,0:T(8,128)}, f32[2,16,768]{2,1,0:T(8,128)}) custom-call(f32[2,16,768]{2,1,0:T(8,128)S(1)} %get-tuple-element.4.res, f32[2,16,768]{2,1,0:T(8,128)S(1)} %get-tuple-element.5.upd), custom_call_target="tpu_custom_call" | custom-call | tf_op jit(solution)/shard_map/pallas_call | solution.py:514
